TPU v7x, 256 devices: a whole 4x4x8 slice. The times are simulated.
256 devices in a mesh: rows: 64 (over z, x, core), coil: 4 (over y).
Axes of the slice: x: 4, y: 4, z: 8, core: 2. Of those that a mesh axis runs over, the one named last changes fastest.
Arguments:
- kspace: float32 [128, 32768], P('coil', 'rows'), may hold values from -6 to 6
- sample_mask: int32 [128, 32768], P('coil', 'rows'), may hold values 0 or 1
- start_basis: float32 [4, 2048, 128], P('coil', 'rows'), may hold values from -6 to 6
Outputs:
- recovered: float32 [128, 32768], P('coil', 'rows')
- basis: float32 [4, 2048, 128], P('coil', 'rows')
All inputs are finite; a program needn't handle non-finite values. No bound on the sum of `sample_mask` on one device may be relied on, other than what follows from the above.
Results may differ from a plain program's by a relative error of at most 0.00011.
Values sent between devices are 32-bit elements; how exact they have to be, the bound alone decides.
A program may use at most 64 MiB of HBM per device.

v0:
```python
import jax
import jax.numpy as jnp
from jax import lax
from jax.sharding import PartitionSpec as P

KER = 64
ITERS = 2
threshold = 0.05


def shifted(block, axis, distance):
    devices = range(lax.axis_size(axis))
    route = [((i - distance) % len(devices), i) for i in devices]
    return lax.ppermute(block, axis, route)


def orthonormal(normal_rows, gram_matrix):
    factor = jnp.linalg.cholesky(gram_matrix)
    return lax.linalg.triangular_solve(
        factor, normal_rows, left_side=False, lower=True, transpose_a=True
    )


def coil_total(partial_value):
    return lax.psum(partial_value, "coil")


def shards(kspace, sample_mask, start_basis):
    highest = lax.Precision.HIGHEST
    channels = kspace.shape[0]
    tile_rows = kspace.shape[1]
    mask_float = sample_mask.astype(jnp.float32)
    sampled = kspace * mask_float
    next_rim = shifted(sampled[:, : KER - 1], "rows", -1)
    extended = jnp.concatenate([sampled, next_rim], axis=1)
    hankel_cols = jnp.stack(
        [extended[:, offset : offset + tile_rows] for offset in range(KER)], axis=0
    )
    hankel_cols = hankel_cols.reshape(KER * channels, tile_rows)
    owned_basis = start_basis.reshape(start_basis.shape[1], start_basis.shape[2])

    def fold_basis(shard_piece):
        return lax.dot_general(
            shard_piece,
            hankel_cols,
            (((0,), (0,)), ((), ())),
            precision=highest,
            preferred_element_type=jnp.float32,
        )

    def apply_hankel(current):
        partial_value = fold_basis(lax.all_gather(current, "rows", axis=0, tiled=True))
        return coil_total(partial_value)

    for iteration in range(ITERS):
        images = apply_hankel(owned_basis)
        normal_rows = lax.psum_scatter(
            lax.dot_general(
                hankel_cols,
                images,
                (((1,), (1,)), ((), ())),
                precision=highest,
                preferred_element_type=jnp.float32,
            ),
            "rows",
            scatter_dimension=0,
            tiled=True,
        )
        local_gram = jnp.dot(
            normal_rows.T, normal_rows, precision=highest, preferred_element_type=jnp.float32
        )
        gram_matrix = lax.psum(local_gram, ("rows", "coil"))
        owned_basis = orthonormal(normal_rows, gram_matrix)
    images = apply_hankel(owned_basis)
    projected = jnp.dot(
        lax.all_gather(owned_basis, "rows", axis=0, tiled=True),
        images,
        precision=highest,
        preferred_element_type=jnp.float32,
    )
    stacked = projected.reshape(KER, channels, tile_rows)
    spread = jnp.zeros((channels, tile_rows + KER - 1), jnp.float32)
    for offset in range(KER):
        spread = spread.at[:, offset : offset + tile_rows].add(stacked[offset])
    carried = shifted(spread[:, tile_rows:], "rows", 1)
    estimate = spread[:, :tile_rows].at[:, : KER - 1].add(carried) / KER
    residual = mask_float * (kspace - estimate)
    recovered = estimate + residual - jnp.clip(residual, -threshold, threshold)
    return (recovered, owned_basis.reshape(1, owned_basis.shape[0], owned_basis.shape[1]))


def solution(mesh):
    return jax.shard_map(
        shards,
        mesh=mesh,
        in_specs=(P("coil", "rows"), P("coil", "rows"), P("coil", "rows", None)),
        out_specs=(P("coil", "rows"), P("coil", "rows", None)),
        check_vma=False,
    )
```

profile of v0, /device:TPU:16, one launch (start us, length us, event | category | flops | bytes accessed | tf_op | source)
XLA Modules:
  0.0 1392.1 jit_solution(3663720347566413571)
XLA Ops:
  8.7 7.5 collective-permute-start
  62.2 28.1 %all-gather.9.cloned.1.call-done = f32[1,2048,128]{2,1,0:T(8,128)} async-done(((f32[1,32,128]{2,1,0:T(8,128)}), f32[1,2048,128]{2,1,0:T(8,128)}) %all-gather.9.cloned.1.call-update) | async-done | bytes 1048592 | tf_op jit(solution)/shard_map/all_gather | solution.py:52
  90.4 9.9 convolution_bitcast_fusion
  100.5 43.9 %all-reduce.7.cloned.1.call-done = f32[128,512]{0,1:T(8,128)} async-done(((f32[128,512]{0,1:T(8,128)}), f32[128,512]{0,1:T(8,128)}) %all-reduce.7.cloned.1.call-update) | async-done | bytes 262160 | tf_op jit(solution)/shard_map/psum | solution.py:25
  144.4 6.6 fusion.135
  151.0 141.7 %reduce-scatter.3.cloned.1.call-done = f32[32,128]{1,0:T(8,128)} async-done(((f32[2048,128]{1,0:T(8,128)}), f32[32,128]{1,0:T(8,128)}) %reduce-scatter.3.cloned.1.call-update) | async-done | bytes 16400 | tf_op jit(solution)/shard_map/reduce_scatter | solution.py:57
  292.7 1.7 fusion.136
  294.5 243.0 %all-reduce.9.cloned.1.call-done = f32[128,128]{0,1:T(8,128)} async-done(((f32[128,128]{0,1:T(8,128)}), f32[128,128]{0,1:T(8,128)}) %all-reduce.9.cloned.1.call-update) | async-done | bytes 65552 | tf_op jit(solution)/shard_map/psum | solution.py:72
  539.3 11.7 cholesky.44
  552.3 9.8 custom-call.6
  563.9 74.0 %all-gather.5.cloned.1.call-done = f32[2048,128]{1,0:T(8,128)} async-done(((f32[32,128]{1,0:T(8,128)}), f32[2048,128]{1,0:T(8,128)}) %all-gather.5.cloned.1.call-update) | async-done | bytes 1048592 | tf_op jit(solution)/shard_map/all_gather | solution.py:52
  637.9 5.8 fusion.137
  643.8 44.0 %all-reduce.11.cloned.1.call-done = f32[128,512]{1,0:T(8,128)} async-done(((f32[128,512]{1,0:T(8,128)}), f32[128,512]{1,0:T(8,128)}) %all-reduce.11.cloned.1.call-update) | async-done | bytes 262160 | tf_op jit(solution)/shard_map/psum | solution.py:25
  687.9 6.6 fusion.138
  694.6 141.7 %reduce-scatter.5.cloned.1.call-done = f32[32,128]{1,0:T(8,128)} async-done(((f32[2048,128]{1,0:T(8,128)}), f32[32,128]{1,0:T(8,128)}) %reduce-scatter.5.cloned.1.call-update) | async-done | bytes 16400 | tf_op jit(solution)/shard_map/reduce_scatter | solution.py:57
  836.3 1.7 fusion.139
  838.5 242.7 %all-reduce.13.cloned.1.call-done = f32[128,128]{0,1:T(8,128)} async-done(((f32[128,128]{0,1:T(8,128)}), f32[128,128]{0,1:T(8,128)}) %all-reduce.13.cloned.1.call-update) | async-done | bytes 65552 | tf_op jit(solution)/shard_map/psum | solution.py:72
  1083.0 11.7 cholesky.55
  1096.0 9.8 custom-call.7
  1107.4 74.2 %all-gather.7.cloned.1.call-done = f32[2048,128]{1,0:T(8,128)} async-done(((f32[32,128]{1,0:T(8,128)}), f32[2048,128]{1,0:T(8,128)}) %all-gather.7.cloned.1.call-update) | async-done | bytes 1048592 | tf_op jit(solution)/shard_map/all_gather | solution.py:76
  1181.6 5.9 fusion.140
  1231.7 4.5 fusion.141
  1321.9 1.6 add_select_fusion.23
  1378.1 5.2 collective-permute-done.1
  (304 shorter events, 243.0 us)
Async XLA Ops:
  7.2 83.2 %all-gather.9.cloned.1.call-start = ((), (), s32[]{:S(2)}) async-start(), calls=%async_computation.11 | async-start | bytes 1064960 | tf_op jit(solution)/shard_map/all_gather | solution.py:52
  8.7 8.9 collective-permute-start
  16.2 128.1 %all-reduce.7.cloned.1.call-start = ((), (), s32[]{:S(2)}) async-start(), calls=%async_computation.2 | async-start | bytes 524288 | tf_op jit(solution)/shard_map/psum | solution.py:25
  100.3 192.4 %reduce-scatter.3.cloned.1.call-start = ((), (), s32[]{:S(2)}) async-start(), calls=%async_computation.3 | async-start | bytes 1064960 | tf_op jit(solution)/shard_map/reduce_scatter | solution.py:57
  151.0 386.5 %all-reduce.9.cloned.1.call-start = ((), (), s32[]{:S(2)}) async-start(), calls=%async_computation.4 | async-start | bytes 131072 | tf_op jit(solution)/shard_map/psum | solution.py:72
  294.4 343.5 %all-gather.5.cloned.1.call-start = ((), (), s32[]{:S(2)}) async-start(), calls=%async_computation.5 | async-start | bytes 1064960 | tf_op jit(solution)/shard_map/all_gather | solution.py:52
  563.7 124.2 %all-reduce.11.cloned.1.call-start = ((), (), s32[]{:S(2)}) async-start(), calls=%async_computation.6 | async-start | bytes 524288 | tf_op jit(solution)/shard_map/psum | solution.py:25
  643.8 192.5 %reduce-scatter.5.cloned.1.call-start = ((), (), s32[]{:S(2)}) async-start(), calls=%async_computation.7 | async-start | bytes 1064960 | tf_op jit(solution)/shard_map/reduce_scatter | solution.py:57
  694.5 386.7 %all-reduce.13.cloned.1.call-start = ((), (), s32[]{:S(2)}) async-start(), calls=%async_computation.8 | async-start | bytes 131072 | tf_op jit(solution)/shard_map/psum | solution.py:72
  838.0 343.6 %all-gather.7.cloned.1.call-start = ((), (), s32[]{:S(2)}) async-start(), calls=%async_computation.9 | async-start | bytes 1064960 | tf_op jit(solution)/shard_map/all_gather | solution.py:76
  1107.4 124.3 %all-reduce.15.cloned.1.call-start = ((), (), s32[]{:S(2)}) async-start(), calls=%async_computation.10 | async-start | bytes 524288 | tf_op jit(solution)/shard_map/psum | solution.py:25
  1181.6 50.0 %copy-start.1 = (f32[2048,128]{1,0:T(8,128)S(1)}, f32[2048,128]{1,0:T(8,128)}, u32[]{:S(2)}) copy-start(f32[2048,128]{1,0:T(8,128)} %all-gather.7.cloned.1.call-done) | copy-start | bytes 3145732
  1236.1 2.0 copy-start
  1321.9 62.4 %copy-start.2 = (f32[32,512]{1,0:T(8,128)S(1)}, f32[32,512]{1,0:T(8,128)}, u32[]{:S(2)}) copy-start(f32[32,512]{1,0:T(8,128)} %param.136) | copy-start | bytes 196612
  1321.9 62.4 %copy-start.3 = (s32[32,512]{1,0:T(8,128)S(1)}, s32[32,512]{1,0:T(8,128)}, u32[]{:S(2)}) copy-start(s32[32,512]{1,0:T(8,128)} %param.137) | copy-start | bytes 196612
  1376.8 6.5 collective-permute-start.1
Sparse Core Ops, SparseCore 0:
  16.4 73.9 all-gather.8
  100.4 43.9 all-reduce.6
  151.1 141.5 reduce-scatter.2
  298.6 238.8 all-reduce.8
  563.8 74.1 all-gather.4
  643.9 43.9 all-reduce.10
  694.6 141.5 reduce-scatter.4
  842.3 238.8 all-reduce.12
  1107.5 74.1 all-gather.6
  1187.7 43.9 all-reduce.14
where the time goes:
time: 1400 us; the launch traced here: 1390 us
  waiting for transfers between devices  1040 us (74%)
  other arithmetic  234 us (17%)
  local copies, waits for them, and re-layouts  46 us (3%)
  matrix products  45.7 us (3%)
  between operations  15.6 us (1%)
    psum x2, waiting for transfers between devices, shards(): gram_matrix = lax.psum(local_gram, ('rows', 'coil'))  486 us
    reduce_scatter x2, waiting for transfers between devices, shards(): lax.psum_scatter(lax.dot_general(hankel_cols, images, (((1,), (1,)), ((),...  283 us
    another operation x128, other arithmetic  139 us
    all_gather x2, waiting for transfers between devices, apply_hankel(): lax.all_gather(current, 'rows', axis=0, tiled=True)  102 us
    psum x3, waiting for transfers between devices, coil_total(): return lax.psum(partial_value, 'coil')  89.5 us
    all_gather x1, waiting for transfers between devices, shards(): lax.all_gather(owned_basis, 'rows', axis=0, tiled=True)  74.2 us
    unnamed x63, other arithmetic  45.3 us
    scatter-add x64, local copies, waits for them, and re-layouts, shards(): spread = spread.at[:, offset:offset + tile_rows].add(stacked[offset])  43.2 us
  transfers between devices with their start and end apart: 12, of which 12 were waited for; matrix products, arithmetic and copies ran while one was open for 6% of the time, Pallas kernels for 0%

commit v1 on v0

--- a/solution.py
+++ b/solution.py
@@ -6,6 +6,11 @@
 KER = 64
 ITERS = 2
 threshold = 0.05
+
+
+def one_after_other(array, first, second):
+    half = lax.psum(array, first)
+    return lax.psum(half, second)
 
 
 def shifted(block, axis, distance):
@@ -69,7 +74,7 @@
         local_gram = jnp.dot(
             normal_rows.T, normal_rows, precision=highest, preferred_element_type=jnp.float32
         )
-        gram_matrix = lax.psum(local_gram, ("rows", "coil"))
+        gram_matrix = one_after_other(local_gram, "coil", "rows")
         owned_basis = orthonormal(normal_rows, gram_matrix)
     images = apply_hankel(owned_basis)
     projected = jnp.dot(

time: 1400 us -> 1360 us (0.971)
  waiting for transfers between devices: 1040 us -> 995 us
    psum x2 -> x4, waiting for transfers between devices: 486 us -> 440 us  [the longest x2 350 us: one_after_other(): return lax.psum(half, second)]
  transfers between devices with their start and end apart: 12 -> 14, of which waited for: 12 -> 14; matrix products, arithmetic and copies ran while one was open for 6% -> 7% of each run, Pallas kernels for 0% -> 0%
where the time goes in v1:
time: 1360 us; the launch traced here: 1350 us
  waiting for transfers between devices  995 us (73%)
  other arithmetic  234 us (17%)
  local copies, waits for them, and re-layouts  46 us (3%)
  matrix products  45.7 us (3%)
  between operations  15.7 us (1%)
    psum x2, waiting for transfers between devices, one_after_other(): return lax.psum(half, second)  350 us
    reduce_scatter x2, waiting for transfers between devices, shards(): lax.psum_scatter(lax.dot_general(hankel_cols, images, (((1,), (1,)), ((),...  283 us
    another operation x128, other arithmetic  139 us
    all_gather x2, waiting for transfers between devices, apply_hankel(): lax.all_gather(current, 'rows', axis=0, tiled=True)  102 us
    psum x3, waiting for transfers between devices, coil_total(): return lax.psum(partial_value, 'coil')  89.5 us
    psum x2, waiting for transfers between devices, one_after_other(): half = lax.psum(array, first)  89.5 us
    all_gather x1, waiting for transfers between devices, shards(): lax.all_gather(owned_basis, 'rows', axis=0, tiled=True)  73.9 us
    unnamed x63, other arithmetic  45.3 us
  transfers between devices with their start and end apart: 14, of which 14 were waited for; matrix products, arithmetic and copies ran while one was open for 7% of the time, Pallas kernels for 0%

profile of v1, /device:TPU:16, one launch (start us, length us, event | category | flops | bytes accessed | tf_op | source)
XLA Modules:
  0.0 1345.6 jit_solution(18267408769081180647)
XLA Ops:
  8.7 7.5 collective-permute-start
  62.2 28.1 %all-gather.9.cloned.1.call-done = f32[1,2048,128]{2,1,0:T(8,128)} async-done(((f32[1,32,128]{2,1,0:T(8,128)}), f32[1,2048,128]{2,1,0:T(8,128)}) %all-gather.9.cloned.1.call-update) | async-done | bytes 1048592 | tf_op jit(solution)/shard_map/all_gather | solution.py:57
  90.4 9.9 convolution_bitcast_fusion
  100.5 43.9 %all-reduce.9.cloned.1.call-done = f32[128,512]{0,1:T(8,128)} async-done(((f32[128,512]{0,1:T(8,128)}), f32[128,512]{0,1:T(8,128)}) %all-reduce.9.cloned.1.call-update) | async-done | bytes 262160 | tf_op jit(solution)/shard_map/psum | solution.py:30
  144.4 6.6 fusion.135
  151.0 141.7 %reduce-scatter.3.cloned.1.call-done = f32[32,128]{1,0:T(8,128)} async-done(((f32[2048,128]{1,0:T(8,128)}), f32[32,128]{1,0:T(8,128)}) %reduce-scatter.3.cloned.1.call-update) | async-done | bytes 16400 | tf_op jit(solution)/shard_map/reduce_scatter | solution.py:62
  294.5 44.7 %all-reduce.11.cloned.1.call-done = f32[128,128]{0,1:T(8,128)} async-done(((f32[128,128]{0,1:T(8,128)}), f32[128,128]{0,1:T(8,128)}) %all-reduce.11.cloned.1.call-update) | async-done | bytes 65552 | tf_op jit(solution)/shard_map/psum | solution.py:12
  339.2 175.4 %all-reduce.13.cloned.1.call-done = f32[128,128]{0,1:T(8,128)} async-done(((f32[128,128]{0,1:T(8,128)}), f32[128,128]{0,1:T(8,128)}) %all-reduce.13.cloned.1.call-update) | async-done | bytes 65552 | tf_op jit(solution)/shard_map/psum | solution.py:13
  516.4 11.7 cholesky.44
  529.4 9.8 custom-call.6
  541.0 73.7 %all-gather.5.cloned.1.call-done = f32[2048,128]{1,0:T(8,128)} async-done(((f32[32,128]{1,0:T(8,128)}), f32[2048,128]{1,0:T(8,128)}) %all-gather.5.cloned.1.call-update) | async-done | bytes 1048592 | tf_op jit(solution)/shard_map/all_gather | solution.py:57
  614.7 5.8 fusion.137
  620.6 44.0 %all-reduce.15.cloned.1.call-done = f32[128,512]{1,0:T(8,128)} async-done(((f32[128,512]{1,0:T(8,128)}), f32[128,512]{1,0:T(8,128)}) %all-reduce.15.cloned.1.call-update) | async-done | bytes 262160 | tf_op jit(solution)/shard_map/psum | solution.py:30
  664.6 6.6 fusion.138
  671.3 141.7 %reduce-scatter.5.cloned.1.call-done = f32[32,128]{1,0:T(8,128)} async-done(((f32[2048,128]{1,0:T(8,128)}), f32[32,128]{1,0:T(8,128)}) %reduce-scatter.5.cloned.1.call-update) | async-done | bytes 16400 | tf_op jit(solution)/shard_map/reduce_scatter | solution.py:62
  813.0 1.7 fusion.139
  814.8 44.8 %all-reduce.17.cloned.1.call-done = f32[128,128]{0,1:T(8,128)} async-done(((f32[128,128]{0,1:T(8,128)}), f32[128,128]{0,1:T(8,128)}) %all-reduce.17.cloned.1.call-update) | async-done | bytes 65552 | tf_op jit(solution)/shard_map/psum | solution.py:12
  860.1 174.9 %all-reduce.19.cloned.1.call-done = f32[128,128]{0,1:T(8,128)} async-done(((f32[128,128]{0,1:T(8,128)}), f32[128,128]{0,1:T(8,128)}) %all-reduce.19.cloned.1.call-update) | async-done | bytes 65552 | tf_op jit(solution)/shard_map/psum | solution.py:13
  1036.8 11.7 cholesky.55
  1049.9 9.8 custom-call.7
  1061.2 73.9 %all-gather.7.cloned.1.call-done = f32[2048,128]{1,0:T(8,128)} async-done(((f32[32,128]{1,0:T(8,128)}), f32[2048,128]{1,0:T(8,128)}) %all-gather.7.cloned.1.call-update) | async-done | bytes 1048592 | tf_op jit(solution)/shard_map/all_gather | solution.py:81
  1135.1 5.9 fusion.140
  1185.2 4.5 fusion.141
  1331.6 5.2 collective-permute-done.1
  (310 shorter events, 246.4 us)
Async XLA Ops:
  7.2 83.2 %all-gather.9.cloned.1.call-start = ((), (), s32[]{:S(2)}) async-start(), calls=%async_computation.13 | async-start | bytes 1064960 | tf_op jit(solution)/shard_map/all_gather | solution.py:57
  8.7 8.9 collective-permute-start
  16.2 128.1 %all-reduce.9.cloned.1.call-start = ((), (), s32[]{:S(2)}) async-start(), calls=%async_computation.2 | async-start | bytes 524288 | tf_op jit(solution)/shard_map/psum | solution.py:30
  100.3 192.4 %reduce-scatter.3.cloned.1.call-start = ((), (), s32[]{:S(2)}) async-start(), calls=%async_computation.3 | async-start | bytes 1064960 | tf_op jit(solution)/shard_map/reduce_scatter | solution.py:62
  151.0 188.2 %all-reduce.11.cloned.1.call-start = ((), (), s32[]{:S(2)}) async-start(), calls=%async_computation.4 | async-start | bytes 131072 | tf_op jit(solution)/shard_map/psum | solution.py:12
  294.4 220.1 %all-reduce.13.cloned.1.call-start = ((), (), s32[]{:S(2)}) async-start(), calls=%async_computation.5 | async-start | bytes 131072 | tf_op jit(solution)/shard_map/psum | solution.py:13
  339.2 275.5 %all-gather.5.cloned.1.call-start = ((), (), s32[]{:S(2)}) async-start(), calls=%async_computation.6 | async-start | bytes 1064960 | tf_op jit(solution)/shard_map/all_gather | solution.py:57
  540.8 123.8 %all-reduce.15.cloned.1.call-start = ((), (), s32[]{:S(2)}) async-start(), calls=%async_computation.7 | async-start | bytes 524288 | tf_op jit(solution)/shard_map/psum | solution.py:30
  620.5 192.5 %reduce-scatter.5.cloned.1.call-start = ((), (), s32[]{:S(2)}) async-start(), calls=%async_computation.8 | async-start | bytes 1064960 | tf_op jit(solution)/shard_map/reduce_scatter | solution.py:62
  671.3 188.3 %all-reduce.17.cloned.1.call-start = ((), (), s32[]{:S(2)}) async-start(), calls=%async_computation.9 | async-start | bytes 131072 | tf_op jit(solution)/shard_map/psum | solution.py:12
  814.7 220.3 %all-reduce.19.cloned.1.call-start = ((), (), s32[]{:S(2)}) async-start(), calls=%async_computation.10 | async-start | bytes 131072 | tf_op jit(solution)/shard_map/psum | solution.py:13
  859.6 275.5 %all-gather.7.cloned.1.call-start = ((), (), s32[]{:S(2)}) async-start(), calls=%async_computation.11 | async-start | bytes 1064960 | tf_op jit(solution)/shard_map/all_gather | solution.py:81
  1061.2 124.0 %all-reduce.21.cloned.1.call-start = ((), (), s32[]{:S(2)}) async-start(), calls=%async_computation.12 | async-start | bytes 524288 | tf_op jit(solution)/shard_map/psum | solution.py:30
  1135.1 50.0 %copy-start.1 = (f32[2048,128]{1,0:T(8,128)S(1)}, f32[2048,128]{1,0:T(8,128)}, u32[]{:S(2)}) copy-start(f32[2048,128]{1,0:T(8,128)} %all-gather.7.cloned.1.call-done) | copy-start | bytes 3145732
  1189.6 2.0 copy-start
  1275.4 62.4 %copy-start.2 = (f32[32,512]{1,0:T(8,128)S(1)}, f32[32,512]{1,0:T(8,128)}, u32[]{:S(2)}) copy-start(f32[32,512]{1,0:T(8,128)} %param.136) | copy-start | bytes 196612
  1275.4 62.4 %copy-start.3 = (s32[32,512]{1,0:T(8,128)S(1)}, s32[32,512]{1,0:T(8,128)}, u32[]{:S(2)}) copy-start(s32[32,512]{1,0:T(8,128)} %param.137) | copy-start | bytes 196612
  1330.3 6.5 collective-permute-start.1
Sparse Core Ops, SparseCore 0:
  16.4 73.9 all-gather.8
  100.4 43.9 all-reduce.8
  151.1 141.5 reduce-scatter.2
  295.4 43.6 all-reduce.10
  342.5 172.0 all-reduce.12
  540.9 73.7 all-gather.4
  620.6 43.9 all-reduce.14
  671.4 141.5 reduce-scatter.4
  815.9 43.6 all-reduce.16
  862.9 172.0 all-reduce.18
  1061.3 73.7 all-gather.6
  1141.2 43.9 all-reduce.20
